TPU v7x, 512 devices: a whole 4x8x8 slice. The times are simulated.
512 devices in a mesh: grp: 16 (over y, x_lo), blk: 32 (over z, x_hi, core).
Axes of the slice: x: 4 (x_hi: 2, x_lo: 2; x = x_hi * 2 + x_lo), y: 8, z: 8, core: 2. Of those that a mesh axis runs over, the one named last changes fastest.
Arguments:
- amplitudes: float32 [128, 128, 2048], P('blk', None, 'grp'), may hold values from -6 to 6
- ladder_ints: float32 [2048, 2048], P('grp', 'blk'), may hold values from -0.375 to 0.375
- cycle_ints: float32 [2048, 2048], P('grp', 'blk'), may hold values from -0.375 to 0.375
- occ_coupling: float32 [128, 128], replicated, may hold values from -1.5 to 1.5
- occ_irrep: int32 [128], replicated, may hold values from 0 to 7
- pair_irrep: int32 [16], replicated, may hold values from 0 to 7
- screen: int32 [16, 16], replicated, may hold values 0 or 1
- block_order: int32 [16], replicated, may hold values from 0 to 15, each once
Outputs:
- residual: float32 [128, 128, 2048], P('blk', None, 'grp')
Inputs may be any that keep to these rules, and one draw needn't show every extreme that they name: block_order names every block once.
All inputs are finite; a program needn't handle non-finite values.
Results may differ from a plain program's by a relative error of at most 0.000071.
Values sent between devices are 32-bit elements; how exact they have to be, the bound alone decides.
A program may use at most 64 MiB of HBM per device.

v0:
```python
import jax
import jax.numpy as jnp
from jax import lax
from jax.sharding import PartitionSpec as P


def shards(
    amplitudes, ladder_ints, cycle_ints, occ_coupling, occ_irrep, pair_irrep, screen, block_order
):
    highest = lax.Precision.HIGHEST
    rows_i, occ, cols_g = amplitudes.shape
    nblocks = pair_irrep.shape[0]
    blk_grp = nblocks // lax.axis_size("grp")
    tile = cols_g // blk_grp
    grp_id = lax.axis_index("grp")
    row_id = lax.axis_index("blk")
    my_occ = lax.dynamic_slice_in_dim(occ_irrep, row_id * rows_i, rows_i)
    my_labels = lax.dynamic_slice_in_dim(pair_irrep, grp_id * blk_grp, blk_grp)
    my_screen = lax.dynamic_slice_in_dim(screen, grp_id * blk_grp, blk_grp, 0).astype(jnp.float32)
    pair_sym = jnp.bitwise_xor(my_occ[:, None], occ_irrep[None, :])
    amp_mask = (pair_sym[:, :, None] == my_labels[None, None, :]).astype(jnp.float32)
    amps3 = (amplitudes.reshape(rows_i, occ, blk_grp, tile) * amp_mask[:, :, :, None]).reshape(
        rows_i, occ, cols_g
    )
    amps = amps3.reshape(rows_i * occ, cols_g)
    coupling = occ_coupling * (occ_irrep[:, None] == occ_irrep[None, :]).astype(jnp.float32)
    label_cols = pair_irrep.astype(jnp.float32)[None, :]
    mine_rows = my_labels.astype(jnp.float32)[:, None]
    local_panels = jnp.stack((ladder_ints, cycle_ints))
    piece = lax.all_gather(local_panels, "blk", axis=2, tiled=True)
    count = piece.shape[2]
    col_blk = jnp.arange(count, dtype=jnp.int32) // tile
    onehot = (col_blk[None, :] == jnp.arange(nblocks, dtype=jnp.int32)[:, None]).astype(jnp.float32)
    col_lab = jnp.dot(label_cols, onehot, precision=highest)
    same = (mine_rows == col_lab).astype(jnp.float32)
    kept = jnp.dot(my_screen, onehot, precision=highest)
    keep_ladder = same * kept
    ladder_panel = (piece[0].reshape(blk_grp, tile, count) * keep_ladder[:, None, :]).reshape(
        cols_g, count
    )
    cycle_panel = (piece[1].reshape(blk_grp, tile, count) * same[:, None, :]).reshape(cols_g, count)
    ladder = jnp.dot(amps, ladder_panel, precision=highest, preferred_element_type=jnp.float32)
    inner = jnp.dot(amps, cycle_panel, precision=highest, preferred_element_type=jnp.float32)
    cycle = jnp.einsum(
        "ikx,kj->ijx", inner.reshape(rows_i, occ, count), coupling, precision=highest
    )
    partial_value = ladder + cycle.reshape(rows_i * occ, count)
    ordered = jnp.take(partial_value.reshape(rows_i, occ, nblocks, tile), block_order, axis=2)
    ordered = ordered.reshape(rows_i, occ, nblocks * tile)
    moved = lax.all_to_all(ordered, "blk", split_axis=1, concat_axis=0, tiled=True)
    anti = ordered - jnp.transpose(moved, (1, 0, 2))
    result = lax.psum_scatter(anti, "grp", scatter_dimension=2, tiled=True)
    return result


def solution(mesh):
    placed = (P("blk", None, "grp"), P("grp", "blk"), P("grp", "blk"), P(), P(), P(), P(), P())
    return jax.shard_map(
        shards, mesh=mesh, in_specs=placed, out_specs=P("blk", None, "grp"), check_vma=False
    )
```

profile of v0, /device:TPU:18, one launch (start us, length us, event | category | flops | bytes accessed | tf_op | source)
XLA Modules:
  0.0 363.0 jit_solution(6302833797781969086)
XLA Ops:
  6.5 0.0 all-gather.2.cloned.1.call-start
  6.5 1.4 pad_maximum_fusion
  8.0 0.0 all-gather.2.cloned.1.call-update
  8.0 0.0 reduce-scatter.2.cloned.1.call-start
  8.1 1.3 dynamic_slice.10
  10.1 0.9 fusion.8
  10.9 0.8 fusion.9
  11.8 0.7 dynamic_slice.9
  12.5 0.7 compare_select_fusion
  13.2 0.7 compare_and_fusion
  13.9 0.1 broadcast_bitcast_fusion
  13.9 1.4 fusion.22
  15.3 1.1 broadcast_multiply_fusion
  16.4 84.0 %all-gather.2.cloned.1.call-done = f32[2,128,2048]{1,2,0:T(8,128)} async-done(((f32[2,128,64]{1,2,0:T(8,128)}), f32[2,128,2048]{1,2,0:T(8,128)}) %all-gather.2.cloned.1.call-update) | async-done | bytes 2097168 | tf_op jit(solution)/shard_map/all_gather | solution.py:30
  100.4 4.8 %fusion.2 = f32[4,128,2048]{2,1,0:T(8,128)S(1)} fusion(f32[4,128,128]{2,1,0:T(8,128)S(1)} %broadcast_multiply_fusion, f32[2,128,2048]{1,2,0:T(8,128)} %all-gather.2.cloned.1.call-done, f32[2048]{0:T(1024)S(1)} %convert_element_type.28), kind=kOutput, calls=%fused_computation.7 | convolution fusion | flops 1610874880 | bytes 5513216 | tf_op jit(solution)/shard_map/dot_general | solution.py:43
  105.3 0.0 copy-done.2
  105.3 0.0 copy-done.1
  105.3 4.1 %fusion.10 = f32[128,4,2048]{2,0,1:T(8,128)S(1)} fusion(f32[4,128,2048]{2,1,0:T(8,128)S(1)} %fusion.2, f32[128,128]{1,0:T(8,128)S(1)} %copy-done.1, s32[128]{0:T(128)S(1)} %copy-done.2), kind=kOutput, calls=%fused_computation.17 | convolution fusion | flops 1610645504 | bytes 8454656 | tf_op jit(solution)/shard_map/ikx,kj->ijx/dot_general | solution.py:44
  109.4 3.6 %fusion = f32[64,8,16,128]{3,1,2,0:T(8,128)S(1)} fusion(f32[128,4,2048]{2,0,1:T(8,128)S(1)} %fusion.10, f32[512,128]{1,0:T(8,128)S(1)} %bitcast.55, f32[2,128,2048]{1,2,0:T(8,128)S(1)} %copy-done, f32[2048]{0:T(1024)S(1)} %get-tuple-element.5), kind=kOutput, calls=%fused_computation.4 | convolution fusion | flops 1611923456 | bytes 9707520 | tf_op jit(solution)/shard_map/dot_general | solution.py:42
  113.0 1.1 copy.40
  114.2 3.2 copy.30
  117.4 5.0 %gather_fusion = f32[16,4,128,128]{3,2,1,0:T(8,128)} fusion(f32[4,128,16,128]{3,1,2,0:T(8,128)} %copy.30, s32[1024]{0:T(1024)S(1)} %pad_clamp_fusion), kind=kCustom, calls=%fused_computation | custom fusion | bytes 8388672 | tf_op jit(solution)/shard_map/jit(_take)/gather | solution.py:48
  122.4 5.3 %copy.31 = f32[4,128,16,128]{1,3,2,0:T(8,128)} copy(f32[4,128,16,128]{3,1,0,2:T(8,128)} %bitcast.51) | data formatting | bytes 8388608 | tf_op jit(solution)/shard_map/jit(_take)/gather | solution.py:48
  127.7 3.8 %bitcast_select_fusion = f32[4,128,2048]{1,2,0:T(8,128)} fusion(f32[4,128,16,128]{1,3,2,0:T(8,128)} %copy.31, pred[2048]{0:T(1024)(128)(4,1)S(1)} %broadcast_bitcast_fusion), kind=kLoop, calls=%fused_computation.3 | loop fusion | flops 1048576 | bytes 8390656 | tf_op jit(solution)/shard_map/jit(_take)/select_n | solution.py:48
  131.5 5.5 %copy.32 = f32[4,128,2048]{2,0,1:T(4,128)} copy(f32[4,128,2048]{1,2,0:T(8,128)} %bitcast_select_fusion) | data formatting | bytes 8388608 | tf_op jit(solution)/shard_map/jit(_take)/select_n | solution.py:48
  137.0 101.9 %all_to_all.18 = f32[4,128,2048]{2,0,1:T(4,128)S(1)} all-to-all(f32[4,128,2048]{2,0,1:T(4,128)} %copy.32), channel_id=1, replica_groups=mesh['grp'=16,'blk'=32] {'blk'}, dimensions={1} | all-to-all | bytes 8388608 | tf_op jit(solution)/shard_map/all_to_all | solution.py:50
  238.9 5.5 %copy.33 = f32[32,4,4,2048]{3,2,1,0:T(4,128)} copy(f32[32,4,4,2048]{3,1,2,0:T(4,128)S(1)} %bitcast.53) | data formatting | bytes 8388608 | tf_op jit(solution)/shard_map/all_to_all | solution.py:50
  244.5 5.3 %copy.34 = f32[128,4,2048]{0,2,1:T(8,128)} copy(f32[128,4,2048]{2,1,0:T(4,128)} %bitcast.54) | data formatting | bytes 8388608 | tf_op jit(solution)/shard_map/all_to_all | solution.py:50
  249.8 5.1 %bitcast_subtract_fusion = f32[4,128,2048]{1,2,0:T(8,128)} fusion(f32[128,4,2048]{0,2,1:T(8,128)} %copy.34, f32[4,128,16,128]{1,3,2,0:T(8,128)} %copy.31, pred[2048]{0:T(1024)(128)(4,1)S(1)} %broadcast_bitcast_fusion), kind=kLoop, calls=%fused_computation.2 | loop fusion | flops 2097152 | bytes 12584960 | tf_op jit(solution)/shard_map/sub | solution.py:51
  254.8 0.0 reduce-scatter.2.cloned.1.call-update
  254.8 99.5 %reduce-scatter.2.cloned.1.call-done = f32[4,128,128]{1,2,0:T(8,128)} async-done(((f32[4,128,2048]{1,2,0:T(8,128)}), f32[4,128,128]{1,2,0:T(8,128)}) %reduce-scatter.2.cloned.1.call-update) | async-done | bytes 262160 | tf_op jit(solution)/shard_map/reduce_scatter | solution.py:52
  354.3 1.8 copy.35
  (8 shorter events, 0.0 us)
Async XLA Ops:
  6.5 98.7 %copy-start.2 = (s32[128]{0:T(128)S(1)}, s32[128]{0:T(128)}, u32[]{:S(2)}) copy-start(s32[128]{0:T(128)} %param.12) | copy-start | bytes 1540
  6.5 98.7 %copy-start.1 = (f32[128,128]{1,0:T(8,128)S(1)}, f32[128,128]{1,0:T(8,128)}, u32[]{:S(2)}) copy-start(f32[128,128]{1,0:T(8,128)} %param.11) | copy-start | bytes 196612
  6.5 93.9 %all-gather.2.cloned.1.call-start = ((), (), s32[]{:S(2)}) async-start(), calls=%async_computation.2 | async-start | bytes 2162688 | tf_op jit(solution)/shard_map/all_gather | solution.py:30
  8.0 346.3 %reduce-scatter.2.cloned.1.call-start = ((), (), s32[]{:S(2)}) async-start(), calls=%async_computation.3 | async-start | bytes 4456448 | tf_op jit(solution)/shard_map/reduce_scatter | solution.py:52
  105.3 4.1 %copy-start = (f32[2,128,2048]{1,2,0:T(8,128)S(1)}, f32[2,128,2048]{1,2,0:T(8,128)}, u32[]{:S(2)}) copy-start(f32[2,128,2048]{1,2,0:T(8,128)} %all-gather.2.cloned.1.call-done) | copy-start | bytes 6291460
Sparse Core Ops, SparseCore 0:
  10.8 89.6 all-gather.1
  255.0 99.3 reduce-scatter.1
where the time goes:
time: 364 us; the launch traced here: 363 us
  waiting for transfers between devices  184 us (51%)
  blocking collectives  102 us (28%)
  local copies, waits for them, and re-layouts  34.9 us (10%)
  matrix products  14.2 us (4%)
  between operations  14.2 us (4%)
  other arithmetic  14.1 us (4%)
    all_to_all x1, blocking collectives, shards(): lax.all_to_all(ordered, 'blk', split_axis=1, concat_axis=0, tiled=True)  102 us
    reduce_scatter x1, waiting for transfers between devices, shards(): result = lax.psum_scatter(anti, 'grp', scatter_dimension=2, tiled=True)  99.5 us
    all_gather x1, waiting for transfers between devices, shards(): piece = lax.all_gather(local_panels, 'blk', axis=2, tiled=True)  84 us
    all_to_all x2, local copies, waits for them, and re-layouts, shards(): lax.all_to_all(ordered, 'blk', split_axis=1, concat_axis=0, tiled=True)  10.8 us
    gather x2, local copies, waits for them, and re-layouts, shards(): jnp.take(partial_value.reshape(rows_i, occ, nblocks, tile), block_order,...  10.3 us
  transfers between devices with their start and end apart: 2, of which 2 were waited for; matrix products, arithmetic and copies ran while one was open for 2% of the time, Pallas kernels for 0%

commit v1 on v0

--- a/solution.py
+++ b/solution.py
@@ -27,7 +27,9 @@
     label_cols = pair_irrep.astype(jnp.float32)[None, :]
     mine_rows = my_labels.astype(jnp.float32)[:, None]
     local_panels = jnp.stack((ladder_ints, cycle_ints))
-    piece = lax.all_gather(local_panels, "blk", axis=2, tiled=True)
+    piece = jnp.concatenate(
+        lax.all_to_all(jnp.stack([local_panels] * lax.axis_size("blk")), "blk", 0, 0), axis=2
+    )
     count = piece.shape[2]
     col_blk = jnp.arange(count, dtype=jnp.int32) // tile
     onehot = (col_blk[None, :] == jnp.arange(nblocks, dtype=jnp.int32)[:, None]).astype(jnp.float32)

time: 364 us -> 335 us (0.920)
  waiting for transfers between devices: 184 us -> 147 us
  starting transfers between devices: 0.04 us -> 12.3 us
    all_gather x1 -> x0, waiting for transfers between devices: 84 us -> none  [shards(): piece = lax.all_gather(local_panels, 'blk', axis=2, tiled=True)]
    all_to_all x0 -> x1, waiting for transfers between devices: none -> 46.8 us  [shards(): lax.all_to_all(jnp.stack([local_panels] * lax.axis_size('blk')), 'blk', 0...]
    all_to_all x0 -> x1, starting transfers between devices: none -> 12.3 us  [shards(): lax.all_to_all(jnp.stack([local_panels] * lax.axis_size('blk')), 'blk', 0...]
  transfers between devices with their start and end apart: 2 -> 2, of which waited for: 2 -> 2; matrix products, arithmetic and copies ran while one was open for 2% -> 1% of each run, Pallas kernels for 0% -> 0%
where the time goes in v1:
time: 335 us
  waiting for transfers between devices  147 us (44%)
  blocking collectives  103 us (31%)
  local copies, waits for them, and re-layouts  35.5 us (11%)
  between operations  14.2 us (4%)
  starting transfers between devices  12.3 us (4%)
  matrix products  12.2 us (4%)
  other arithmetic  11.3 us (3%)
    all_to_all x1, blocking collectives, shards(): lax.all_to_all(ordered, 'blk', split_axis=1, concat_axis=0, tiled=True)  103 us
    reduce_scatter x1, waiting for transfers between devices, shards(): result = lax.psum_scatter(anti, 'grp', scatter_dimension=2, tiled=True)  99.9 us
    all_to_all x1, waiting for transfers between devices, shards(): lax.all_to_all(jnp.stack([local_panels] * lax.axis_size('blk')), 'blk', 0...  46.8 us
    all_to_all x1, starting transfers between devices, shards(): lax.all_to_all(jnp.stack([local_panels] * lax.axis_size('blk')), 'blk', 0...  12.3 us
    all_to_all x2, local copies, waits for them, and re-layouts, shards(): lax.all_to_all(ordered, 'blk', split_axis=1, concat_axis=0, tiled=True)  10.8 us
    gather x2, local copies, waits for them, and re-layouts, shards(): jnp.take(partial_value.reshape(rows_i, occ, nblocks, tile), block_order,...  10.3 us
  transfers between devices with their start and end apart: 2, of which 2 were waited for; matrix products, arithmetic and copies ran while one was open for 1% of the time, Pallas kernels for 0%

profile of v1, /device:TPU:18, one launch (start us, length us, event | category | flops | bytes accessed | tf_op | source)
XLA Modules:
  0.0 334.7 jit_solution(8411419126447753994)
XLA Ops:
  6.5 0.8 pad_maximum_fusion
  7.4 1.6 stack.11
  9.0 12.3 %all-to-all-start = ((f32[32,2,128,64]{2,3,1,0:T(8,128)}), f32[32,2,128,64]{2,3,1,0:T(8,128)S(1)}, u32[]{:S(2)}, u32[]{:S(2)}) async-start(f32[32,2,128,64]{2,3,1,0:T(8,128)} %stack.11), calls=%async_computation | async-start | bytes 4194304 | tf_op jit(solution)/shard_map/all_to_all | solution.py:31
  21.2 0.0 reduce-scatter.2.cloned.1.call-start
  21.3 0.6 dynamic_slice.10
  22.6 0.9 fusion.1
  23.4 0.2 fusion.2
  23.6 0.1 mul.56
  23.7 0.1 reshape.151
  23.8 0.1 dynamic_slice.9
  23.9 0.1 broadcast_bitcast_fusion
  23.9 0.7 fusion.15
  24.7 0.1 broadcast_multiply_fusion
  24.8 46.8 %all-to-all-done = f32[32,2,128,64]{2,3,1,0:T(8,128)S(1)} async-done(((f32[32,2,128,64]{2,3,1,0:T(8,128)}), f32[32,2,128,64]{2,3,1,0:T(8,128)S(1)}, u32[]{:S(2)}, u32[]{:S(2)}) %all-to-all-start) | async-done | bytes 2097184 | tf_op jit(solution)/shard_map/all_to_all | solution.py:31
  71.6 0.2 copy.44
  71.8 0.7 slice_multiply_fusion.1
  72.5 3.5 %fusion.19 = f32[4,128,2048]{2,1,0:T(8,128)S(1)} fusion(f32[4,128,128]{2,1,0:T(8,128)S(1)} %broadcast_multiply_fusion, f32[128,2048,1]{0,1,2:T(8,128)S(1)} %bitcast.58), kind=kOutput, calls=%fused_computation.42 | convolution fusion | flops 1610612736 | bytes 5505024 | tf_op jit(solution)/shard_map/dot_general | solution.py:45
  76.1 4.1 %fusion.3 = f32[128,4,2048]{2,0,1:T(8,128)S(1)} fusion(f32[4,128,2048]{2,1,0:T(8,128)S(1)} %fusion.19, f32[128,128]{1,0:T(8,128)S(1)} %copy-done.1, s32[128]{0:T(128)S(1)} %copy-done.2), kind=kOutput, calls=%fused_computation.13 | convolution fusion | flops 1610645504 | bytes 8454656 | tf_op jit(solution)/shard_map/ikx,kj->ijx/dot_general | solution.py:46
  80.2 3.6 %fusion = f32[64,8,16,128]{3,1,2,0:T(8,128)S(1)} fusion(f32[128,4,2048]{2,0,1:T(8,128)S(1)} %fusion.3, f32[512,128]{1,0:T(8,128)S(1)} %bitcast.59, f32[128,2048]{0,1:T(8,128)S(1)} %bitcast.57), kind=kOutput, calls=%fused_computation.4 | convolution fusion | flops 1611661312 | bytes 9699328 | tf_op jit(solution)/shard_map/dot_general | solution.py:44
  83.7 0.9 copy.42
  84.6 3.4 %copy.32 = f32[4,128,16,128]{3,1,2,0:T(8,128)} copy(f32[4,128,16,128]{3,2,1,0:T(8,128)S(1)} %bitcast.53) | data formatting | bytes 8388608 | tf_op jit(solution)/shard_map/reshape | solution.py:50
  88.1 5.0 %gather_fusion = f32[16,4,128,128]{3,2,1,0:T(8,128)} fusion(f32[4,128,16,128]{3,1,2,0:T(8,128)} %copy.32, s32[1024]{0:T(1024)S(1)} %pad_clamp_fusion), kind=kCustom, calls=%fused_computation | custom fusion | bytes 8388672 | tf_op jit(solution)/shard_map/jit(_take)/gather | solution.py:50
  93.0 5.3 %copy.33 = f32[4,128,16,128]{1,3,2,0:T(8,128)} copy(f32[4,128,16,128]{3,1,0,2:T(8,128)} %bitcast.52) | data formatting | bytes 8388608 | tf_op jit(solution)/shard_map/jit(_take)/gather | solution.py:50
  98.4 3.8 %bitcast_select_fusion = f32[4,128,2048]{1,2,0:T(8,128)} fusion(f32[4,128,16,128]{1,3,2,0:T(8,128)} %copy.33, pred[2048]{0:T(1024)(128)(4,1)S(1)} %broadcast_bitcast_fusion), kind=kLoop, calls=%fused_computation.3 | loop fusion | flops 1048576 | bytes 8390656 | tf_op jit(solution)/shard_map/jit(_take)/select_n | solution.py:50
  102.2 5.5 %copy.34 = f32[4,128,2048]{2,0,1:T(4,128)} copy(f32[4,128,2048]{1,2,0:T(8,128)} %bitcast_select_fusion) | data formatting | bytes 8388608 | tf_op jit(solution)/shard_map/jit(_take)/select_n | solution.py:50
  107.7 102.6 %all_to_all.23 = f32[4,128,2048]{2,0,1:T(4,128)S(1)} all-to-all(f32[4,128,2048]{2,0,1:T(4,128)} %copy.34), channel_id=1, replica_groups=mesh['grp'=16,'blk'=32] {'blk'}, dimensions={1} | all-to-all | bytes 8388608 | tf_op jit(solution)/shard_map/all_to_all | solution.py:52
  210.3 5.5 %copy.35 = f32[32,4,4,2048]{3,2,1,0:T(4,128)} copy(f32[32,4,4,2048]{3,1,2,0:T(4,128)S(1)} %bitcast.54) | data formatting | bytes 8388608 | tf_op jit(solution)/shard_map/all_to_all | solution.py:52
  215.8 5.3 %copy.36 = f32[128,4,2048]{0,2,1:T(8,128)} copy(f32[128,4,2048]{2,1,0:T(4,128)} %bitcast.55) | data formatting | bytes 8388608 | tf_op jit(solution)/shard_map/all_to_all | solution.py:52
  221.1 5.0 %bitcast_subtract_fusion = f32[4,128,2048]{1,2,0:T(8,128)} fusion(f32[128,4,2048]{0,2,1:T(8,128)} %copy.36, f32[4,128,16,128]{1,3,2,0:T(8,128)} %copy.33, pred[2048]{0:T(1024)(128)(4,1)S(1)} %broadcast_bitcast_fusion), kind=kLoop, calls=%fused_computation.2 | loop fusion | flops 2097152 | bytes 12584960 | tf_op jit(solution)/shard_map/sub | solution.py:53
  226.1 0.0 reduce-scatter.2.cloned.1.call-update
  226.1 99.9 %reduce-scatter.2.cloned.1.call-done = f32[4,128,128]{1,2,0:T(8,128)} async-done(((f32[4,128,2048]{1,2,0:T(8,128)}), f32[4,128,128]{1,2,0:T(8,128)}) %reduce-scatter.2.cloned.1.call-update) | async-done | bytes 262160 | tf_op jit(solution)/shard_map/reduce_scatter | solution.py:54
  326.1 1.8 copy.37
  (16 shorter events, 0.1 us)
Async XLA Ops:
  6.5 14.8 %copy-start.3 = (s32[16]{0:T(128)S(1)}, s32[16]{0:T(128)}, u32[]{:S(2)}) copy-start(s32[16]{0:T(128)} %param.13) | copy-start | bytes 196
  6.5 17.2 %copy-start.2 = (s32[128]{0:T(128)S(1)}, s32[128]{0:T(128)}, u32[]{:S(2)}) copy-start(s32[128]{0:T(128)} %param.12) | copy-start | bytes 1540
  6.5 17.3 %copy-start.4 = (s32[16]{0:T(128)S(1)}, s32[16]{0:T(128)}, u32[]{:S(2)}) copy-start(s32[16]{0:T(128)} %param.15) | copy-start | bytes 196
  6.5 18.1 %copy-start = (f32[4,128,128]{2,1,0:T(8,128)S(1)}, f32[4,128,128]{2,1,0:T(8,128)}, u32[]{:S(2)}) copy-start(f32[4,128,128]{2,1,0:T(8,128)} %param.8) | copy-start | bytes 786436
  9.0 62.6 %all-to-all-start = ((f32[32,2,128,64]{2,3,1,0:T(8,128)}), f32[32,2,128,64]{2,3,1,0:T(8,128)S(1)}, u32[]{:S(2)}, u32[]{:S(2)}) async-start(f32[32,2,128,64]{2,3,1,0:T(8,128)} %stack.11), calls=%async_computation | async-start | bytes 4194304 | tf_op jit(solution)/shard_map/all_to_all | solution.py:31
  21.2 304.8 %reduce-scatter.2.cloned.1.call-start = ((), (), s32[]{:S(2)}) async-start(), calls=%async_computation.3 | async-start | bytes 4456448 | tf_op jit(solution)/shard_map/reduce_scatter | solution.py:54
  71.8 4.2 %copy-start.1 = (f32[128,128]{1,0:T(8,128)S(1)}, f32[128,128]{1,0:T(8,128)}, u32[]{:S(2)}) copy-start(f32[128,128]{1,0:T(8,128)} %param.11) | copy-start | bytes 196612
Sparse Core Ops, SparseCore 0:
  226.3 99.7 reduce-scatter.1
